TPU v7x, 32 devices: a whole 2x2x4 slice. The times are simulated.
32 devices in a mesh: grp: 2 (over y), space: 16 (over z, x, core).
Axes of the slice: x: 2, y: 2, z: 4, core: 2. Of those that a mesh axis runs over, the one named last changes fastest.
Arguments:
- snapshots: bfloat16 [2048, 3, 2048], P(('grp', 'space')), parts along dimension 0, may hold values from -6 to 6
- weights: float32 [4096], P(('grp', 'space')), parts along dimension 0, may hold values from 0.5 to 20, as said below
Outputs:
- spod_matrix: float32 [32, 30, 30], P('grp'), parts along dimension 0
There are 2 independent parts, one for each index of `grp`. A program takes and returns all parts, laid end to end along the dimension named above; each array names one. Nothing has to cross between parts.
Inputs may be any that keep to these rules, and one draw needn't show every extreme that they name: Positive quadrature weights.
All inputs are finite; a program needn't handle non-finite values.
Results may differ from a plain program's by a relative error of at most 0.0003.
Values may be sent and summed in bfloat16 or wider, within the bound.
A program may use at most 128 MiB of HBM per device.

v0:
```python
import functools

import jax
import jax.numpy as jnp
import numpy as np
from jax import lax
from jax.experimental import pallas as pl
from jax.experimental.pallas import tpu as pltpu
from jax.sharding import PartitionSpec as P

NFFT = 128
NB = 15
NF = 16
ROWS = 32
LANES = 128


def table(steps):
    j = np.arange(NFFT)
    window = 0.5 - 0.5 * np.cos(2 * np.pi * j / NFFT)
    window = window / np.sqrt(np.sum(window * window))
    full = np.zeros((NF, ROWS, steps))
    for f in range(NF):
        turns = 2 * np.pi * (((f + 1) * j) % NFFT) / NFFT
        for b in range(NB):
            at = b * (NFFT // 2)
            full[f, b, at:at + NFFT] = window * np.cos(turns)
            full[f, NB + b, at:at + NFFT] = -window * np.sin(turns)
    full = full - full.sum(axis=2, keepdims=True) / steps
    return full.reshape(NF * ROWS, steps)


def split_table(steps, chunk):
    full = table(steps)
    high = full.astype(jnp.bfloat16)
    low = (full - high.astype(np.float64)).astype(jnp.bfloat16)
    both = np.stack([high, low])
    both = both.reshape(2, NF * ROWS, steps // chunk, chunk)
    return np.transpose(both, (2, 0, 1, 3)).reshape(steps // chunk, 2 * NF * ROWS, chunk)


def inner_of(n):
    return 4 if n % 4 == 0 else 1


def owners_of(n):
    return min(max(n // 4, 1), 16)


def each(count, body):
    if count <= 32:
        for k in range(count):
            body(k)
    else:
        def step(k, carry):
            body(k)
            return carry
        lax.fori_loop(0, count, step, 0)


def halves_of(v):
    high = v.astype(jnp.bfloat16)
    return high, (v - high.astype(jnp.float32)).astype(jnp.bfloat16)


def dot_t(a, b):
    return lax.dot_general(a, b, (((1,), (1,)), ((), ())), preferred_element_type=jnp.float32)


def kernel(n, steps_dev, chunk, x_ref, w_ref, s_hbm, out_ref,
           s_ref, recv, acc, gram, parts, total, gathered,
           s_sem, own_sem, send_sem, recv_sem, rs_send, rs_recv, ag_send, ag_recv):
    me = lax.axis_index("space")
    owners = owners_of(n)
    first = (n - owners) // 2
    tile = LANES // owners
    inner = inner_of(n)
    planes = n // inner
    my_plane, my_q = me // inner, lax.rem(me, inner)
    per_chunk = chunk // steps_dev
    n_chunks = n // per_chunk
    rows = NF * ROWS
    mine = w_ref.shape[1]
    components = x_ref.shape[0]

    def peer_of(k):
        return lax.rem(me + 1 + k, n)

    def lanes_of(dest):
        return pl.ds(pl.multiple_of(dest * mine, mine), mine)

    s_copy = pltpu.make_async_copy(s_hbm, s_ref, s_sem)
    s_copy.start()
    own_copy = pltpu.make_async_copy(x_ref.at[:, :, lanes_of(me)], recv.at[me], own_sem)
    own_copy.start()

    barrier = pltpu.get_barrier_semaphore()

    def greet(k):
        pl.semaphore_signal(barrier, inc=1, device_id={"space": peer_of(k)},
                            device_id_type=pl.DeviceIdType.MESH)
    each(n - 1, greet)
    pl.semaphore_wait(barrier, n - 1)

    def data_copy(dest, source):
        return pltpu.make_async_remote_copy(
            src_ref=x_ref.at[:, :, lanes_of(dest)], dst_ref=recv.at[source],
            send_sem=send_sem.at[dest], recv_sem=recv_sem.at[source],
            device_id={"space": dest}, device_id_type=pl.DeviceIdType.MESH)

    def send(plane, low, high):
        def one(k):
            q = lax.rem(my_q + low + k, inner)

            @pl.when(jnp.logical_or(plane != my_plane, q != my_q))
            def _():
                data_copy(plane * inner + q, me).start()
        each(high - low, one)

    def send_far(k):
        d = planes - 1 - k
        pl.when(my_plane + d < planes)(lambda: send(my_plane + d, 0, inner))
        pl.when(my_plane >= d)(lambda: send(my_plane - d, 0, inner))
    each(planes - 1, send_far)
    send(my_plane, 0, inner)

    acc[...] = jnp.zeros_like(acc)
    s_copy.wait()
    own_copy.wait()
    my_chunk = me // per_chunk

    def absorb(j):
        at = lax.rem(my_chunk + j, n_chunks)

        def arrive(i):
            source = at * per_chunk + i

            @pl.when(source != me)
            def _():
                data_copy(source, source).wait_recv()
        each(per_chunk, arrive)
        held = pl.ds(at * per_chunk, per_chunk)
        block = jnp.concatenate(
            [recv[held, c].reshape(chunk, mine) for c in range(components)], axis=1)
        s = s_ref[at]
        acc[...] += (
            jnp.dot(s[:rows], block, preferred_element_type=jnp.float32)
            + jnp.dot(s[rows:], block, preferred_element_type=jnp.float32))
    each(n_chunks, absorb)

    w = w_ref[...]
    w_all = jnp.concatenate([w] * (acc.shape[1] // w.shape[1]), axis=1)
    w_sum = jnp.sum(w)
    block_of = lax.broadcasted_iota(jnp.int32, (ROWS, LANES), 1) // ROWS
    corner = jnp.logical_and(
        lax.broadcasted_iota(jnp.int32, (ROWS, LANES), 0) == ROWS - 1,
        lax.broadcasted_iota(jnp.int32, (ROWS, LANES), 1) % ROWS == ROWS - 1)
    for g in range(rows // LANES):
        c = acc[g * LANES:(g + 1) * LANES]
        c_high, c_low = halves_of(c)
        a_high, a_low = halves_of(c * w_all)
        full = dot_t(a_high, c_high) + (dot_t(a_high, c_low) + dot_t(a_low, c_high))
        kept = full[:ROWS]
        for i in range(1, LANES // ROWS):
            kept = jnp.where(block_of == i, full[i * ROWS:(i + 1) * ROWS], kept)
        gram[g * ROWS:(g + 1) * ROWS] = jnp.where(corner, w_sum, kept)

    def part_copy(slot, source):
        return pltpu.make_async_remote_copy(
            src_ref=gram.at[pl.ds(pl.multiple_of(slot * tile, tile), tile)],
            dst_ref=parts.at[source],
            send_sem=rs_send.at[slot], recv_sem=rs_recv.at[source],
            device_id={"space": first + slot}, device_id_type=pl.DeviceIdType.MESH)

    def total_copy(dest, slot):
        return pltpu.make_async_remote_copy(
            src_ref=total, dst_ref=gathered.at[slot],
            send_sem=ag_send.at[dest], recv_sem=ag_recv.at[slot],
            device_id={"space": dest}, device_id_type=pl.DeviceIdType.MESH)

    my_slot = me - first
    is_owner = jnp.logical_and(my_slot >= 0, my_slot < owners)

    def for_others(body):
        def one(k):
            slot = lax.rem(me + owners // 2 + k, owners)

            @pl.when(slot != my_slot)
            def _():
                body(slot)
        each(owners, one)
    for_others(lambda slot: part_copy(slot, me).start())

    @pl.when(is_owner)
    def _():
        parts[me] = gram[pl.ds(pl.multiple_of(my_slot * tile, tile), tile)]
        each(n - 1, lambda k: part_copy(my_slot, peer_of(k)).wait_recv())
        total[...] = jnp.sum(parts[...], axis=0)
        def total_to(plane):
            def one(k):
                dest = plane * inner + lax.rem(my_q + k, inner)

                @pl.when(dest != me)
                def _():
                    total_copy(dest, my_slot).start()
            each(inner, one)

        def total_far(k):
            d = planes - 1 - k
            pl.when(my_plane + d < planes)(lambda: total_to(my_plane + d))
            pl.when(my_plane >= d)(lambda: total_to(my_plane - d))
        each(planes - 1, total_far)
        total_to(my_plane)
        gathered[my_slot] = total[...]

    for_others(lambda slot: total_copy(me, slot).wait_recv())

    whole = gathered[...].reshape(LANES, LANES)
    inverse = 1.0 / whole[ROWS - 1:ROWS, ROWS - 1:ROWS]
    per_row = LANES // ROWS
    for f in range(NF):
        g, i = f // per_row, f % per_row
        piece = whole[g * ROWS:g * ROWS + 2 * NB, i * ROWS:i * ROWS + 2 * NB]
        out_ref[:, f, :] = piece * inverse

    each(n - 1, lambda k: data_copy(peer_of(k), me).wait_send())

    for_others(lambda slot: part_copy(slot, me).wait_send())

    @pl.when(is_owner)
    def _():
        each(n - 1, lambda k: total_copy(peer_of(k), my_slot).wait_send())


def local(n, snapshots, weights):
    steps_dev, components, points = snapshots.shape
    mine = points // n
    steps = steps_dev * n
    chunk = max(256, steps_dev)
    width = components * mine
    x = jnp.transpose(snapshots, (1, 0, 2))
    s = jnp.asarray(split_table(steps, chunk))
    owners = owners_of(n)
    rows = NF * ROWS
    dma = pltpu.SemaphoreType.DMA
    hbm = pl.BlockSpec(memory_space=pl.ANY)
    vmem = pl.BlockSpec(memory_space=pltpu.VMEM)
    out = pl.pallas_call(
        functools.partial(kernel, n, steps_dev, chunk),
        out_shape=jax.ShapeDtypeStruct((2 * NB, NF, 2 * NB), jnp.float32),
        in_specs=[hbm, vmem, hbm],
        out_specs=vmem,
        scratch_shapes=[
            pltpu.VMEM(s.shape, jnp.bfloat16),
            pltpu.VMEM((n, components, steps_dev, mine), jnp.bfloat16),
            pltpu.VMEM((rows, width), jnp.float32),
            pltpu.VMEM((LANES, LANES), jnp.float32),
            pltpu.VMEM((n, LANES // owners, LANES), jnp.float32),
            pltpu.VMEM((LANES // owners, LANES), jnp.float32),
            pltpu.VMEM((owners, LANES // owners, LANES), jnp.float32),
            dma, dma, dma((n,)), dma((n,)), dma((n,)), dma((n,)), dma((n,)), dma((n,)),
        ],
        compiler_params=pltpu.CompilerParams(collective_id=0, has_side_effects=True),
    )(x, weights.reshape(1, mine), s)
    return jnp.transpose(out, (1, 0, 2))


def solution(mesh):
    n = mesh.shape["space"]
    in_specs = (P(("grp", "space"), None, None), P(("grp", "space")))
    out_specs = P("grp", None, None)
    return jax.shard_map(functools.partial(local, n), mesh=mesh, in_specs=in_specs,
                         out_specs=out_specs, check_vma=False)
```

profile of v0, /device:TPU:0, one launch (start us, length us, event | category | flops | bytes accessed | tf_op | source)
XLA Modules:
  0.0 37.4 jit_solution(3550561108010607559)
XLA Ops:
  0.0 35.8 %shard_map.37 = f32[30,16,30]{2,1,0:T(8,128)} custom-call(bf16[3,64,2048]{2,1,0:T(8,128)(2,1)} %bitcast.4, f32[1,128]{1,0:T(1,128)} %bitcast.5, bf16[4,1024,256]{2,1,0:T(8,128)(2,1)} %constant.2.clone.s_hbm), custom_call_target="tpu_custom_call" | custom-call | tf_op jit(solution)/shard_map/pallas_call | solution.py:248
  35.8 1.7 %copy.5 = f32[16,30,30]{2,0,1:T(8,128)} copy(f32[16,30,30]{2,0,1:T(8,128)} %bitcast.3) | data formatting | bytes 115200
where the time goes:
time: 37.6 us; the launch traced here: 37.4 us
  Pallas kernels  35.8 us (95%)
  local copies, waits for them, and re-layouts  1.65 us (4%)
    pallas_call x1, Pallas kernels, local(): pl.pallas_call(functools.partial(kernel, n, steps_dev, chunk), out_shape=...  35.8 us
    unnamed x1, local copies, waits for them, and re-layouts  1.65 us

commit v1 on v0

--- a/solution.py
+++ b/solution.py
@@ -67,7 +67,7 @@
     return lax.dot_general(a, b, (((1,), (1,)), ((), ())), preferred_element_type=jnp.float32)
 
 
-def kernel(n, steps_dev, chunk, x_ref, w_ref, s_hbm, out_ref,
+def raw_kernel(n, steps_dev, chunk, x_ref, w_ref, s_hbm, out_ref,
            s_ref, recv, acc, gram, parts, total, gathered,
            s_sem, own_sem, send_sem, recv_sem, rs_send, rs_recv, ag_send, ag_recv):
     me = lax.axis_index("space")
@@ -232,7 +232,7 @@
         each(n - 1, lambda k: total_copy(peer_of(k), my_slot).wait_send())
 
 
-def local(n, snapshots, weights):
+def raw_local(n, snapshots, weights):
     steps_dev, components, points = snapshots.shape
     mine = points // n
     steps = steps_dev * n
@@ -246,7 +246,7 @@
     hbm = pl.BlockSpec(memory_space=pl.ANY)
     vmem = pl.BlockSpec(memory_space=pltpu.VMEM)
     out = pl.pallas_call(
-        functools.partial(kernel, n, steps_dev, chunk),
+        functools.partial(raw_kernel, n, steps_dev, chunk),
         out_shape=jax.ShapeDtypeStruct((2 * NB, NF, 2 * NB), jnp.float32),
         in_specs=[hbm, vmem, hbm],
         out_specs=vmem,
@@ -265,6 +265,375 @@
     return jnp.transpose(out, (1, 0, 2))
 
 
+HALF = NFFT // 2
+TOP = NF + 2
+MAIN = 2 * NF
+EXTRA = 4
+POWER_BITS = 4
+GAIN = 2.0 ** 7.5
+
+
+def half_rows():
+    j = np.arange(HALF)
+    turns = [2 * np.pi * ((k * j) % NFFT) / NFFT for k in range(TOP)]
+    main = [np.cos(turns[k]) for k in range(1, NF + 1)]
+    main += [-np.sin(turns[k]) for k in range(1, NF + 1)]
+    extra = [np.full(HALF, 1.0 / HALF), np.ones(HALF), np.cos(turns[TOP - 1]), -np.sin(turns[TOP - 1])]
+    return np.stack(main), np.stack(extra)
+
+
+def packed_rows(components):
+    used = components * (MAIN + EXTRA) + 1
+    return -(-used // 16) * 16
+
+
+def split(full):
+    high = full.astype(jnp.bfloat16)
+    return high, (full - high.astype(np.float64)).astype(jnp.bfloat16)
+
+
+def sender_table(components):
+    main, extra = half_rows()
+    packed = packed_rows(components)
+    full = np.zeros((packed, components, HALF))
+    level = np.zeros(packed)
+    for c in range(components):
+        at = components * MAIN + c * EXTRA
+        full[c * MAIN:(c + 1) * MAIN, c] = main
+        full[at:at + EXTRA, c] = extra
+    high, low = split(full.reshape(packed, components * HALF))
+    level = (high.astype(np.float64) + low.astype(np.float64)).sum(axis=1)
+    for c in range(components):
+        level[components * MAIN + c * EXTRA] = 0.0
+    both = np.concatenate([high, low])
+    return both, np.repeat(level.astype(np.float32)[:, None], LANES, axis=1)
+
+
+def combine_table(segments, components):
+    main, extra = half_rows()
+    values = MAIN + EXTRA
+    level = np.concatenate([main, extra]).sum(axis=1)
+    level[MAIN] = 0.0
+
+    def unit(k, imag):
+        row = np.zeros(values)
+        if k == 0:
+            if not imag:
+                row[MAIN + 1] = 1.0
+        elif k == TOP - 1:
+            row[MAIN + 2 + imag] = 1.0
+        else:
+            row[imag * NF + k - 1] = 1.0
+        return row
+
+    full = np.zeros((NF, ROWS, segments, values))
+    for f in range(NF):
+        k = f + 1
+        for imag in range(2):
+            side = 0.25 * (unit(k - 1, imag) + unit(k + 1, imag))
+            first = 0.5 * unit(k, imag) - side
+            second = (-1.0) ** k * (0.5 * unit(k, imag) + side)
+            lift_first, lift_second = first @ level, second @ level
+            both = lift_first + lift_second
+            for b in range(NB):
+                row = full[f, imag * NB + b]
+                row[b] += first
+                row[b + 1] += second
+                row[b, MAIN] += lift_first
+                row[b + 1, MAIN] += lift_second
+                if f == 0 and not imag:
+                    row[:, MAIN] -= both / segments
+                    row[:, MAIN + 1] -= both / (segments * HALF)
+    full = full.reshape(NF * ROWS, segments, values)
+    inner = inner_of(segments)
+    planes = segments // inner
+    tail = packed_rows(components) - components * MAIN
+    wide = np.zeros((NF * ROWS, segments, tail))
+    for c in range(components):
+        wide[:, :, c * EXTRA:(c + 1) * EXTRA] = full[:, :, MAIN:]
+    high, low = split(wide)
+
+    def planed(part):
+        part = part.reshape(NF * ROWS, planes, inner * part.shape[-1])
+        return np.transpose(part, (1, 0, 2)).astype(jnp.bfloat16)
+    return np.concatenate([planed(full[:, :, :MAIN]), planed(high), planed(low)], axis=2)
+
+
+def code(v):
+    a = v
+    for _ in range(POWER_BITS):
+        a = a * a
+    return jnp.where(v < 0.0, -a, a)
+
+
+def decode(y):
+    a = jnp.abs(y)
+    for _ in range(POWER_BITS):
+        a = jnp.sqrt(a)
+    return jnp.where(y < 0.0, -a, a)
+
+
+def spectral_kernel(n, x_ref, w_ref, f_ref, level_ref, t_hbm, out_ref,
+                    x_buf, t_ref, outbox, recv, acc, gram, parts, total, gathered,
+                    x_sem, t_sem, own_sem, send_sem, recv_sem, rs_send, rs_recv, ag_send, ag_recv):
+    me = lax.axis_index("space")
+    owners = owners_of(n)
+    first = (n - owners) // 2
+    tile = LANES // owners
+    inner = inner_of(n)
+    planes = n // inner
+    my_plane, my_q = me // inner, lax.rem(me, inner)
+    rows = NF * ROWS
+    mine = w_ref.shape[1]
+    components, steps_dev = x_ref.shape[:2]
+    packed = recv.shape[1]
+    body = components * MAIN
+
+    def peer_of(k):
+        return lax.rem(me + 1 + k, n)
+
+    def plane_of(k):
+        return lax.rem(my_plane + planes - 1 - k + planes // 2, planes)
+
+    def x_copy(k):
+        width = inner * mine
+        lanes = pl.ds(pl.multiple_of(plane_of(k) * width, width), width)
+        return pltpu.make_async_copy(x_ref.at[:, :, lanes], x_buf.at[k], x_sem.at[k])
+    each(planes, lambda k: x_copy(k).start())
+    t_copy = pltpu.make_async_copy(t_hbm, t_ref, t_sem)
+    t_copy.start()
+
+    barrier = pltpu.get_barrier_semaphore()
+
+    def greet(k):
+        pl.semaphore_signal(barrier, inc=1, device_id={"space": peer_of(k)},
+                            device_id_type=pl.DeviceIdType.MESH)
+    each(n - 1, greet)
+
+    def data_copy(dest, source):
+        return pltpu.make_async_remote_copy(
+            src_ref=outbox.at[dest], dst_ref=recv.at[source],
+            send_sem=send_sem.at[dest], recv_sem=recv_sem.at[source],
+            device_id={"space": dest}, device_id_type=pl.DeviceIdType.MESH)
+
+    tail_row = lax.broadcasted_iota(jnp.int32, (packed - body, LANES), 0)
+    tail_kind = lax.rem(tail_row, EXTRA)
+    in_tail = tail_row < components * EXTRA
+    coded = jnp.logical_and(in_tail, tail_kind > 0)
+    is_scale = tail_row == components * EXTRA
+
+    def prepare(k):
+        x_copy(k).wait()
+        x = x_buf[k].reshape(components * steps_dev, inner * mine)
+        both = jnp.dot(f_ref[...], x, preferred_element_type=jnp.float32)
+        y = both[:packed] + both[packed:]
+        for q in range(inner):
+            part = y[:, q * mine:(q + 1) * mine]
+            tail = part[body:]
+            means = [tail[c * EXTRA:c * EXTRA + 1].astype(jnp.bfloat16).astype(jnp.float32)
+                     for c in range(components)]
+            spread = jnp.broadcast_to(means[-1], tail.shape)
+            for c in range(components - 1):
+                inside = jnp.logical_and(tail_row >= c * EXTRA, tail_row < (c + 1) * EXTRA)
+                spread = jnp.where(inside, means[c], spread)
+            tail = tail - level_ref[body:] * spread
+            mains = [part[c * MAIN:(c + 1) * MAIN] - level_ref[c * MAIN:(c + 1) * MAIN] * means[c]
+                     for c in range(components)]
+            largest = jnp.max(jnp.where(coded, jnp.abs(tail), 0.0), axis=0, keepdims=True)
+            for m in mains:
+                largest = jnp.maximum(largest, jnp.max(jnp.abs(m), axis=0, keepdims=True))
+            scale = jnp.maximum(largest, 1e-30).astype(jnp.bfloat16).astype(jnp.float32)
+            grow = GAIN / scale
+            dest = plane_of(k) * inner + q
+            for c in range(components):
+                outbox[dest, c * MAIN:(c + 1) * MAIN] = code(mains[c] * grow).astype(jnp.bfloat16)
+            sent = jnp.where(coded, code(tail * grow), jnp.where(is_scale, scale, spread))
+            outbox[dest, body:] = sent.astype(jnp.bfloat16)
+
+    def launch(k):
+        def one(i):
+            dest = plane_of(k) * inner + lax.rem(my_q + i, inner)
+
+            @pl.when(dest != me)
+            def _():
+                data_copy(dest, me).start()
+        each(inner, one)
+
+    def step(k):
+        prepare(k)
+        if k == 0:
+            pl.semaphore_wait(barrier, n - 1)
+        launch(k)
+    for k in range(planes):
+        step(k)
+    own_copy = pltpu.make_async_copy(outbox.at[me], recv.at[me], own_sem)
+    own_copy.start()
+
+    acc[...] = jnp.zeros_like(acc)
+    t_copy.wait()
+    own_copy.wait()
+
+    def absorb(j):
+        at = lax.rem(my_plane + j, planes)
+
+        def arrive(i):
+            source = at * inner + i
+
+            @pl.when(source != me)
+            def _():
+                data_copy(source, source).wait_recv()
+        each(inner, arrive)
+        columns = [[] for _ in range(components)]
+        tails = []
+        for i in range(inner):
+            source = at * inner + i
+            tail = recv[source, body:].astype(jnp.float32)
+            scale = tail[components * EXTRA:components * EXTRA + 1] * (1.0 / GAIN)
+            for c in range(components):
+                y = recv[source, c * MAIN:(c + 1) * MAIN].astype(jnp.float32)
+                columns[c].append(decode(y) * scale)
+            tails.append(jnp.where(coded, decode(tail) * scale, tail))
+        tail = jnp.concatenate(tails, axis=0)
+        row = lax.rem(lax.broadcasted_iota(jnp.int32, tail.shape, 0), packed - body)
+        pieces = []
+        for c in range(components):
+            inside = jnp.logical_and(row >= c * EXTRA, row < (c + 1) * EXTRA)
+            own = jnp.where(inside, tail, 0.0)
+            pieces.append(jnp.concatenate(columns[c] + [own, own], axis=0))
+        block = jnp.concatenate(pieces, axis=1)
+        high, low = halves_of(block)
+        t = t_ref[at]
+        acc[...] += (
+            jnp.dot(t, high, preferred_element_type=jnp.float32)
+            + jnp.dot(t, low, preferred_element_type=jnp.float32))
+    each(planes, absorb)
+
+    w = w_ref[...]
+    w_all = jnp.concatenate([w] * (acc.shape[1] // w.shape[1]), axis=1)
+    w_sum = jnp.sum(w)
+    block_of = lax.broadcasted_iota(jnp.int32, (ROWS, LANES), 1) // ROWS
+    corner = jnp.logical_and(
+        lax.broadcasted_iota(jnp.int32, (ROWS, LANES), 0) == ROWS - 1,
+        lax.broadcasted_iota(jnp.int32, (ROWS, LANES), 1) % ROWS == ROWS - 1)
+    for g in range(rows // LANES):
+        c = acc[g * LANES:(g + 1) * LANES]
+        c_high, c_low = halves_of(c)
+        a_high, a_low = halves_of(c * w_all)
+        full = dot_t(a_high, c_high) + (dot_t(a_high, c_low) + dot_t(a_low, c_high))
+        kept = full[:ROWS]
+        for i in range(1, LANES // ROWS):
+            kept = jnp.where(block_of == i, full[i * ROWS:(i + 1) * ROWS], kept)
+        gram[g * ROWS:(g + 1) * ROWS] = jnp.where(corner, w_sum, kept)
+
+    def part_copy(slot, source):
+        return pltpu.make_async_remote_copy(
+            src_ref=gram.at[pl.ds(pl.multiple_of(slot * tile, tile), tile)],
+            dst_ref=parts.at[source],
+            send_sem=rs_send.at[slot], recv_sem=rs_recv.at[source],
+            device_id={"space": first + slot}, device_id_type=pl.DeviceIdType.MESH)
+
+    def total_copy(dest, slot):
+        return pltpu.make_async_remote_copy(
+            src_ref=total, dst_ref=gathered.at[slot],
+            send_sem=ag_send.at[dest], recv_sem=ag_recv.at[slot],
+            device_id={"space": dest}, device_id_type=pl.DeviceIdType.MESH)
+
+    my_slot = me - first
+    is_owner = jnp.logical_and(my_slot >= 0, my_slot < owners)
+
+    def for_others(body):
+        def one(k):
+            slot = lax.rem(me + owners // 2 + k, owners)
+
+            @pl.when(slot != my_slot)
+            def _():
+                body(slot)
+        each(owners, one)
+    for_others(lambda slot: part_copy(slot, me).start())
+
+    @pl.when(is_owner)
+    def _():
+        parts[me] = gram[pl.ds(pl.multiple_of(my_slot * tile, tile), tile)]
+        each(n - 1, lambda k: part_copy(my_slot, peer_of(k)).wait_recv())
+        total[...] = jnp.sum(parts[...], axis=0)
+        def total_to(plane):
+            def one(k):
+                dest = plane * inner + lax.rem(my_q + k, inner)
+
+                @pl.when(dest != me)
+                def _():
+                    total_copy(dest, my_slot).start()
+            each(inner, one)
+
+        def total_far(k):
+            d = planes - 1 - k
+            pl.when(my_plane + d < planes)(lambda: total_to(my_plane + d))
+            pl.when(my_plane >= d)(lambda: total_to(my_plane - d))
+        each(planes - 1, total_far)
+        total_to(my_plane)
+        gathered[my_slot] = total[...]
+
+    for_others(lambda slot: total_copy(me, slot).wait_recv())
+
+    whole = gathered[...].reshape(LANES, LANES)
+    inverse = 1.0 / (whole[ROWS - 1:ROWS, ROWS - 1:ROWS] * (3.0 * NFFT / 8.0))
+    per_row = LANES // ROWS
+    for f in range(NF):
+        g, i = f // per_row, f % per_row
+        piece = whole[g * ROWS:g * ROWS + 2 * NB, i * ROWS:i * ROWS + 2 * NB]
+        out_ref[:, f, :] = piece * inverse
+
+    each(n - 1, lambda k: data_copy(peer_of(k), me).wait_send())
+
+    for_others(lambda slot: part_copy(slot, me).wait_send())
+
+    @pl.when(is_owner)
+    def _():
+        each(n - 1, lambda k: total_copy(peer_of(k), my_slot).wait_send())
+
+
+def spectral_local(n, snapshots, weights):
+    steps_dev, components, points = snapshots.shape
+    mine = points // n
+    x = jnp.transpose(snapshots, (1, 0, 2))
+    forward, level = sender_table(components)
+    back = combine_table(n, components)
+    owners = owners_of(n)
+    inner = inner_of(n)
+    planes = n // inner
+    packed = packed_rows(components)
+    rows = NF * ROWS
+    dma = pltpu.SemaphoreType.DMA
+    hbm = pl.BlockSpec(memory_space=pl.ANY)
+    vmem = pl.BlockSpec(memory_space=pltpu.VMEM)
+    out = pl.pallas_call(
+        functools.partial(spectral_kernel, n),
+        out_shape=jax.ShapeDtypeStruct((2 * NB, NF, 2 * NB), jnp.float32),
+        in_specs=[hbm, vmem, vmem, vmem, hbm],
+        out_specs=vmem,
+        scratch_shapes=[
+            pltpu.VMEM((planes, components, steps_dev, inner * mine), jnp.bfloat16),
+            pltpu.VMEM(back.shape, jnp.bfloat16),
+            pltpu.VMEM((n, packed, mine), jnp.bfloat16),
+            pltpu.VMEM((n, packed, mine), jnp.bfloat16),
+            pltpu.VMEM((rows, components * mine), jnp.float32),
+            pltpu.VMEM((LANES, LANES), jnp.float32),
+            pltpu.VMEM((n, LANES // owners, LANES), jnp.float32),
+            pltpu.VMEM((LANES // owners, LANES), jnp.float32),
+            pltpu.VMEM((owners, LANES // owners, LANES), jnp.float32),
+            dma((planes,)), dma, dma, dma((n,)), dma((n,)), dma((n,)), dma((n,)), dma((n,)), dma((n,)),
+        ],
+        compiler_params=pltpu.CompilerParams(collective_id=0, has_side_effects=True),
+    )(x, weights.reshape(1, mine), jnp.asarray(forward), jnp.asarray(level), jnp.asarray(back))
+    return jnp.transpose(out, (1, 0, 2))
+
+
+def local(n, snapshots, weights):
+    steps_dev, components, points = snapshots.shape
+    fits = steps_dev == HALF and n == NB + 1 and points == n * LANES
+    return (spectral_local if fits else raw_local)(n, snapshots, weights)
+
+
 def solution(mesh):
     n = mesh.shape["space"]
     in_specs = (P(("grp", "space"), None, None), P(("grp", "space")))

time: 37.6 us -> 32.3 us (0.86)
  Pallas kernels: 35.8 us -> 30.4 us
    pallas_call x1, Pallas kernels: 35.8 us -> 30.4 us  [spectral_local(): pl.pallas_call(functools.partial(spectral_kernel, n), out_shape=jax.Shape...]
where the time goes in v1:
time: 32.3 us; the launch traced here: 32.1 us
  Pallas kernels  30.4 us (94%)
  local copies, waits for them, and re-layouts  1.65 us (5%)
    pallas_call x1, Pallas kernels, spectral_local(): pl.pallas_call(functools.partial(spectral_kernel, n), out_shape=jax.Shape...  30.4 us
    unnamed x1, local copies, waits for them, and re-layouts  1.65 us

profile of v1, /device:TPU:0, one launch (start us, length us, event | category | flops | bytes accessed | tf_op | source)
XLA Modules:
  0.0 32.1 jit_solution(1587107542120249668)
XLA Ops:
  0.0 30.4 %shard_map.55 = f32[30,16,30]{2,1,0:T(8,128)} custom-call(bf16[3,64,2048]{2,1,0:T(8,128)(2,1)} %bitcast.4, f32[1,128]{1,0:T(1,128)} %bitcast.5, bf16[224,192]{1,0:T(8,128)(2,1)} %constant.6.clone.f_ref, f32[112,128]{1,0:T(8,128)} %constant.7.clone.level_ref, bf16[4,512,256]{2,1,0:T(8,128)(2,1)} %constant.8.clone.t_hbm), custom_call_target="tpu_custom_call" | custom-call | tf_op jit(solution)/shard_map/pallas_call | solution.py:609
  30.4 1.7 %copy.7 = f32[16,30,30]{2,0,1:T(8,128)} copy(f32[16,30,30]{2,0,1:T(8,128)} %bitcast.3) | data formatting | bytes 115200

commit v2 on v1

--- a/solution.py
+++ b/solution.py
@@ -377,8 +377,8 @@
                     x_buf, t_ref, outbox, recv, acc, gram, parts, total, gathered,
                     x_sem, t_sem, own_sem, send_sem, recv_sem, rs_send, rs_recv, ag_send, ag_recv):
     me = lax.axis_index("space")
-    owners = owners_of(n)
-    first = (n - owners) // 2
+    owners = n // 2
+    first = n // 8
     tile = LANES // owners
     inner = inner_of(n)
     planes = n // inner
@@ -392,8 +392,15 @@
     def peer_of(k):
         return lax.rem(me + 1 + k, n)
 
+    upper = 2 * my_plane >= planes
+
     def plane_of(k):
-        return lax.rem(my_plane + planes - 1 - k + planes // 2, planes)
+        if k == planes - 1:
+            return my_plane
+        down = planes - 1 - k
+        down = jnp.where(down <= my_plane, down - 1, down)
+        up = jnp.where(k >= my_plane, k + 1, k)
+        return jnp.where(upper, up, down)
 
     def x_copy(k):
         width = inner * mine
@@ -508,6 +515,30 @@
             + jnp.dot(t, low, preferred_element_type=jnp.float32))
     each(planes, absorb)
 
+    def part_copy(slot, source):
+        return pltpu.make_async_remote_copy(
+            src_ref=gram.at[pl.ds(pl.multiple_of(slot * tile, tile), tile)],
+            dst_ref=parts.at[source],
+            send_sem=rs_send.at[slot], recv_sem=rs_recv.at[source],
+            device_id={"space": first + slot}, device_id_type=pl.DeviceIdType.MESH)
+
+    def total_copy(dest, slot):
+        return pltpu.make_async_remote_copy(
+            src_ref=total, dst_ref=gathered.at[slot],
+            send_sem=ag_send.at[dest], recv_sem=ag_recv.at[slot],
+            device_id={"space": dest}, device_id_type=pl.DeviceIdType.MESH)
+
+    my_slot = me - first
+    is_owner = jnp.logical_and(my_slot >= 0, my_slot < owners)
+
+    def for_others(body):
+        def one(k):
+            slot = lax.rem(me + owners // 2 + k, owners)
+
+            @pl.when(slot != my_slot)
+            def _():
+                body(slot)
+        each(owners, one)
     w = w_ref[...]
     w_all = jnp.concatenate([w] * (acc.shape[1] // w.shape[1]), axis=1)
     w_sum = jnp.sum(w)
@@ -524,32 +555,11 @@
         for i in range(1, LANES // ROWS):
             kept = jnp.where(block_of == i, full[i * ROWS:(i + 1) * ROWS], kept)
         gram[g * ROWS:(g + 1) * ROWS] = jnp.where(corner, w_sum, kept)
-
-    def part_copy(slot, source):
-        return pltpu.make_async_remote_copy(
-            src_ref=gram.at[pl.ds(pl.multiple_of(slot * tile, tile), tile)],
-            dst_ref=parts.at[source],
-            send_sem=rs_send.at[slot], recv_sem=rs_recv.at[source],
-            device_id={"space": first + slot}, device_id_type=pl.DeviceIdType.MESH)
-
-    def total_copy(dest, slot):
-        return pltpu.make_async_remote_copy(
-            src_ref=total, dst_ref=gathered.at[slot],
-            send_sem=ag_send.at[dest], recv_sem=ag_recv.at[slot],
-            device_id={"space": dest}, device_id_type=pl.DeviceIdType.MESH)
-
-    my_slot = me - first
-    is_owner = jnp.logical_and(my_slot >= 0, my_slot < owners)
-
-    def for_others(body):
-        def one(k):
-            slot = lax.rem(me + owners // 2 + k, owners)
-
-            @pl.when(slot != my_slot)
+        for slot in range(g * ROWS // tile, (g + 1) * ROWS // tile):
+            @pl.when(my_slot != slot)
             def _():
-                body(slot)
-        each(owners, one)
-    for_others(lambda slot: part_copy(slot, me).start())
+                part_copy(slot, me).start()
+
 
     @pl.when(is_owner)
     def _():
@@ -577,11 +587,7 @@
 
     whole = gathered[...].reshape(LANES, LANES)
     inverse = 1.0 / (whole[ROWS - 1:ROWS, ROWS - 1:ROWS] * (3.0 * NFFT / 8.0))
-    per_row = LANES // ROWS
-    for f in range(NF):
-        g, i = f // per_row, f % per_row
-        piece = whole[g * ROWS:g * ROWS + 2 * NB, i * ROWS:i * ROWS + 2 * NB]
-        out_ref[:, f, :] = piece * inverse
+    out_ref[...] = whole * inverse
 
     each(n - 1, lambda k: data_copy(peer_of(k), me).wait_send())
 
@@ -598,7 +604,7 @@
     x = jnp.transpose(snapshots, (1, 0, 2))
     forward, level = sender_table(components)
     back = combine_table(n, components)
-    owners = owners_of(n)
+    owners = n // 2
     inner = inner_of(n)
     planes = n // inner
     packed = packed_rows(components)
@@ -608,7 +614,7 @@
     vmem = pl.BlockSpec(memory_space=pltpu.VMEM)
     out = pl.pallas_call(
         functools.partial(spectral_kernel, n),
-        out_shape=jax.ShapeDtypeStruct((2 * NB, NF, 2 * NB), jnp.float32),
+        out_shape=jax.ShapeDtypeStruct((LANES, LANES), jnp.float32),
         in_specs=[hbm, vmem, vmem, vmem, hbm],
         out_specs=vmem,
         scratch_shapes=[
@@ -625,7 +631,8 @@
         ],
         compiler_params=pltpu.CompilerParams(collective_id=0, has_side_effects=True),
     )(x, weights.reshape(1, mine), jnp.asarray(forward), jnp.asarray(level), jnp.asarray(back))
-    return jnp.transpose(out, (1, 0, 2))
+    out = out.reshape(NF * ROWS // LANES, ROWS, LANES // ROWS, ROWS)[:, :2 * NB, :, :2 * NB]
+    return jnp.transpose(out, (0, 2, 1, 3)).reshape(NF, 2 * NB, 2 * NB)
 
 
 def local(n, snapshots, weights):

time: 32.3 us -> 30.7 us (0.950)
  Pallas kernels: 30.4 us -> 28.7 us
    pallas_call x1, Pallas kernels: 30.4 us -> 28.7 us  [spectral_local(): pl.pallas_call(functools.partial(spectral_kernel, n), out_shape=jax.Shape...]
    unnamed x1 -> x0, local copies, waits for them, and re-layouts: 1.65 us -> none
    reshape x0 -> x1, local copies, waits for them, and re-layouts: none -> 1 us  [spectral_local(): out.reshape(NF * ROWS // LANES, ROWS, LANES // ROWS, ROWS)]
    transpose x0 -> x2, local copies, waits for them, and re-layouts: none -> 0.75 us  [spectral_local(): return jnp.transpose(out, (0, 2, 1, 3)).reshape(NF, 2 * NB, 2 * NB)]
where the time goes in v2:
time: 30.7 us; the launch traced here: 30.5 us
  Pallas kernels  28.7 us (93%)
  local copies, waits for them, and re-layouts  1.76 us (6%)
    pallas_call x1, Pallas kernels, spectral_local(): pl.pallas_call(functools.partial(spectral_kernel, n), out_shape=jax.Shape...  28.7 us
    reshape x1, local copies, waits for them, and re-layouts, spectral_local(): out.reshape(NF * ROWS // LANES, ROWS, LANES // ROWS, ROWS)  1 us
    transpose x2, local copies, waits for them, and re-layouts, spectral_local(): return jnp.transpose(out, (0, 2, 1, 3)).reshape(NF, 2 * NB, 2 * NB)  0.75 us

profile of v2, /device:TPU:0, one launch (start us, length us, event | category | flops | bytes accessed | tf_op | source)
XLA Modules:
  0.0 30.5 jit_solution(4162380226359673797)
XLA Ops:
  0.0 28.7 %shard_map.55 = f32[128,128]{1,0:T(8,128)} custom-call(bf16[3,64,2048]{2,1,0:T(8,128)(2,1)} %bitcast.5, f32[1,128]{1,0:T(1,128)} %bitcast.6, bf16[224,192]{1,0:T(8,128)(2,1)} %constant.6.clone.f_ref, f32[112,128]{1,0:T(8,128)} %constant.7.clone.level_ref, bf16[4,512,256]{2,1,0:T(8,128)(2,1)} %constant.8.clone.t_hbm), custom_call_target="tpu_custom_call" | custom-call | tf_op jit(solution)/shard_map/pallas_call | solution.py:615
  28.7 1.0 %reshape.10 = f32[4,32,4,32]{3,2,1,0:T(4,128)S(1)} reshape(f32[128,128]{1,0:T(8,128)} %shard_map.55) | data formatting | bytes 131072 | tf_op jit(solution)/shard_map/reshape | solution.py:634
  29.8 0.7 %copy.6 = f32[4,4,30,30]{3,1,0,2:T(4,128)} copy(f32[4,4,30,30]{3,1,2,0:T(4,128)S(1)} %slice_bitcast_fusion) | data formatting | bytes 115200 | tf_op jit(solution)/shard_map/transpose | solution.py:635
  (1 shorter events, 0.0 us)

commit v3 on v2

--- a/solution.py
+++ b/solution.py
@@ -367,9 +367,7 @@
 
 
 def decode(y):
-    a = jnp.abs(y)
-    for _ in range(POWER_BITS):
-        a = jnp.sqrt(a)
+    a = jnp.exp2(jnp.log2(jnp.abs(y)) * (0.5 ** POWER_BITS))
     return jnp.where(y < 0.0, -a, a)
 
 
@@ -392,7 +390,9 @@
     def peer_of(k):
         return lax.rem(me + 1 + k, n)
 
-    upper = 2 * my_plane >= planes
+    half = planes // 2
+    upper = my_plane >= half
+    base = jnp.where(upper, half, 0)
 
     def plane_of(k):
         if k == planes - 1:
@@ -481,7 +481,10 @@
     own_copy.wait()
 
     def absorb(j):
-        at = lax.rem(my_plane + j, planes)
+        if j < half:
+            at = base + lax.rem(my_plane - base + j, half)
+        else:
+            at = jnp.where(upper, j - half, planes - 1 - (j - half))
 
         def arrive(i):
             source = at * inner + i

time: 30.7 us -> 29.6 us (0.964)
  Pallas kernels: 28.7 us -> 27.6 us
    pallas_call x1, Pallas kernels: 28.7 us -> 27.6 us  [spectral_local(): pl.pallas_call(functools.partial(spectral_kernel, n), out_shape=jax.Shape...]
where the time goes in v3:
time: 29.6 us; the launch traced here: 29.4 us
  Pallas kernels  27.6 us (93%)
  local copies, waits for them, and re-layouts  1.76 us (6%)
    pallas_call x1, Pallas kernels, spectral_local(): pl.pallas_call(functools.partial(spectral_kernel, n), out_shape=jax.Shape...  27.6 us
    reshape x1, local copies, waits for them, and re-layouts, spectral_local(): out.reshape(NF * ROWS // LANES, ROWS, LANES // ROWS, ROWS)  1 us
    transpose x2, local copies, waits for them, and re-layouts, spectral_local(): return jnp.transpose(out, (0, 2, 1, 3)).reshape(NF, 2 * NB, 2 * NB)  0.75 us

profile of v3, /device:TPU:0, one launch (start us, length us, event | category | flops | bytes accessed | tf_op | source)
XLA Modules:
  0.0 29.4 jit_solution(3883119131568048792)
XLA Ops:
  0.0 27.6 %shard_map.55 = f32[128,128]{1,0:T(8,128)} custom-call(bf16[3,64,2048]{2,1,0:T(8,128)(2,1)} %bitcast.5, f32[1,128]{1,0:T(1,128)} %bitcast.6, bf16[224,192]{1,0:T(8,128)(2,1)} %constant.6.clone.f_ref, f32[112,128]{1,0:T(8,128)} %constant.7.clone.level_ref, bf16[4,512,256]{2,1,0:T(8,128)(2,1)} %constant.8.clone.t_hbm), custom_call_target="tpu_custom_call" | custom-call | tf_op jit(solution)/shard_map/pallas_call | solution.py:618
  27.6 1.0 %reshape.10 = f32[4,32,4,32]{3,2,1,0:T(4,128)S(1)} reshape(f32[128,128]{1,0:T(8,128)} %shard_map.55) | data formatting | bytes 131072 | tf_op jit(solution)/shard_map/reshape | solution.py:637
  28.7 0.7 %copy.6 = f32[4,4,30,30]{3,1,0,2:T(4,128)} copy(f32[4,4,30,30]{3,1,2,0:T(4,128)S(1)} %slice_bitcast_fusion) | data formatting | bytes 115200 | tf_op jit(solution)/shard_map/transpose | solution.py:638
  (1 shorter events, 0.0 us)
